TPU v7x, 512 devices: a whole 4x8x8 slice. The times are simulated.
512 devices in a mesh: rows: 64 (over x, y, z_lo), cols: 8 (over z_hi, core).
Axes of the slice: x: 4, y: 8, z: 8 (z_hi: 4, z_lo: 2; z = z_hi * 2 + z_lo), core: 2. Of those that a mesh axis runs over, the one named last changes fastest.
Arguments:
- design: float32 [65536, 4096], P('rows', 'cols')
- signs: int32 [65536], P('rows'), may hold values from -1 to 1, as said below
- response: float32 [65536], P('rows'), may hold values from -6 to 6
- picks: int32 [8192], replicated, may hold values from 0 to 65535, as said below
Outputs:
- gram_blocks: float32 [512, 8, 512], P('rows', 'cols')
- rhs: float32 [4096], P('cols')
Inputs may be any that keep to these rules, and one draw needn't show every extreme that they name: `signs`: every entry is +1 or -1. `picks`: strictly increasing, all distinct; the first and the last row are always sampled.
All inputs are finite; a program needn't handle non-finite values.
Results may differ from a plain program's by a relative error of at most 0.0003.
Values sent between devices are 32-bit elements; how exact they have to be, the bound alone decides.
A program may use at most 64 MiB of HBM per device.

v0:
```python
import jax
import jax.numpy as jnp
from jax import lax
from jax.sharding import PartitionSpec as P

D = 4096
BW = 512


epsilon = 1e-06


def swapped(block, axis, apart):
    count = lax.axis_size(axis)
    route = []
    for low in range(count):
        high = low | 1 << apart
        if high != low and high < count:
            route += [(low, high), (high, low)]
    return lax.ppermute(block, axis, route)


def sylvester(order):
    row_ids = lax.broadcasted_iota(jnp.int32, (order, order), 0)
    col_ids = lax.broadcasted_iota(jnp.int32, (order, order), 1)
    common = jnp.bitwise_and(row_ids, col_ids)
    parity = jnp.zeros((order, order), jnp.int32)
    for level in range(order.bit_length() - 1):
        parity = jnp.bitwise_xor(parity, jnp.bitwise_and(jnp.right_shift(common, level), 1))
    return (1 - 2 * parity).astype(jnp.float32)


def local_mix(values):
    height = values.shape[0]
    levels = height.bit_length() - 1
    first = 2 ** (levels // 2)
    second = height // first
    folded = values.reshape((first, second) + values.shape[1:])
    folded = jnp.einsum("ab,b...->a...", sylvester(first), folded, precision=lax.Precision.HIGHEST)
    folded = jnp.einsum(
        "jk,ak...->aj...", sylvester(second), folded, precision=lax.Precision.HIGHEST
    )
    return folded.reshape(values.shape)


def local(design, signs, response, picks):
    height = design.shape[0]
    flips = signs.astype(jnp.float32)
    mixed = local_mix(design * flips[:, None])
    answer = local_mix(response * flips)
    groups = lax.axis_size("rows")
    position = lax.axis_index("rows")
    local_ids = lax.iota(jnp.int32, height)
    global_rows = position * height + local_ids
    for section in range(groups.bit_length() - 1):
        other_mixed, other_answer = swapped((mixed, answer), "rows", section)
        is_upper = jnp.bitwise_and(jnp.right_shift(position, section), 1) == 1
        mixed = jnp.where(is_upper, other_mixed - mixed, mixed + other_mixed)
        answer = jnp.where(is_upper, other_answer - answer, answer + other_answer)
    picked = (
        jnp.searchsorted(picks, global_rows, side="right")
        - jnp.searchsorted(picks, global_rows, side="left")
    ).astype(jnp.float32)
    weighted = mixed * picked[:, None]
    trace_part = jnp.sum(weighted * mixed)
    rhs_part = jnp.dot(picked * answer, mixed, precision=lax.Precision.HIGHEST)
    power_part = jnp.sum(picked * answer * answer)
    blocks = mixed.shape[1] // BW
    shaped = mixed.reshape(height, blocks, BW)
    chosen = weighted.reshape(height, blocks, BW)
    gram = lax.psum_scatter(
        jnp.einsum("lbi,lbj->ibj", chosen, shaped, precision=lax.Precision.HIGHEST),
        "rows",
        scatter_dimension=0,
        tiled=True,
    )
    trace_sum = lax.psum(trace_part, ("rows", "cols"))
    rhs_sum, power = lax.psum((rhs_part, power_part), "rows")
    mean_diag = trace_sum / D + epsilon
    samples = picks.shape[0]
    gram_blocks = gram / mean_diag
    rhs = rhs_sum * jnp.sqrt(jnp.float32(samples)) / jnp.sqrt(mean_diag * power)
    return (gram_blocks, rhs)


def solution(mesh):
    in_specs = (P("rows", "cols"), P("rows"), P("rows"), P())
    out_specs = (P("rows", "cols", None), P("cols"))
    return jax.shard_map(local, mesh=mesh, in_specs=in_specs, out_specs=out_specs, check_vma=False)
```

profile of v0, /device:TPU:8, one launch (start us, length us, event | category | flops | bytes accessed | tf_op | source)
XLA Modules:
  0.0 1156.2 jit_solution(6603372293029312399)
XLA Ops:
  16.0 4.3 collective-permute-start
  20.3 45.7 %collective-permute-done = f32[1024,512]{1,0:T(8,128)} collective-permute-done((f32[1024,512]{1,0:T(8,128)S(1)}, f32[1024,512]{1,0:T(8,128)}, u32[]{:S(2)}, u32[]{:S(2)}) %collective-permute-start) | collective-permute-done | bytes 2097184 | tf_op jit(solution)/shard_map/ppermute | solution.py:20
  71.1 46.4 %collective-permute-done.1 = f32[1024,512]{1,0:T(8,128)} collective-permute-done((f32[1024,512]{1,0:T(8,128)S(1)}, f32[1024,512]{1,0:T(8,128)}, u32[]{:S(2)}, u32[]{:S(2)}) %collective-permute-start.1) | collective-permute-done | bytes 2097184 | tf_op jit(solution)/shard_map/ppermute | solution.py:20
  120.2 4.5 collective-permute-start.2
  124.8 88.2 %collective-permute-done.2 = f32[1024,512]{1,0:T(8,128)} collective-permute-done((f32[1024,512]{1,0:T(8,128)S(1)}, f32[1024,512]{1,0:T(8,128)}, u32[]{:S(2)}, u32[]{:S(2)}) %collective-permute-start.2) | collective-permute-done | bytes 2097184 | tf_op jit(solution)/shard_map/ppermute | solution.py:20
  215.7 5.2 collective-permute-start.3
  226.9 5.9 collective-permute-start.7
  232.9 80.1 %collective-permute-done.7 = f32[1024]{0:T(1024)S(1)} collective-permute-done((f32[1024]{0:T(1024)S(1)}, f32[1024]{0:T(1024)S(1)}, u32[]{:S(2)}, u32[]{:S(2)}) %collective-permute-start.7) | collective-permute-done | bytes 4128 | tf_op jit(solution)/shard_map/ppermute | solution.py:20
  315.6 3.8 collective-permute-done.8
  319.4 5.0 collective-permute-start.9
  324.4 4.4 collective-permute-done.9
  328.8 3.5 collective-permute-start.10
  337.6 87.3 %while.48 = (s32[]{:T(128)}, u32[1024]{0:T(1024)S(1)}, u32[1024]{0:T(1024)S(1)}, s32[8192]{0:T(1024)S(1)}, s32[]{:T(128)}, /*index=5*/s32[]{:T(128)}, s32[]{:T(128)}, s32[]{}) while((s32[]{:T(128)}, u32[1024]{0:T(1024)S(1)}, u32[1024]{0:T(1024)S(1)}, s32[8192]{0:T(1024)S(1)}, s32[]{:T(128)}, /*index=5*/s32[]{:T(128)}, s32[]{:T(128)}, ...), condition=%wide.region_1.2_spmd.clone, body=%wide.region_0.1_spmd.clone.sunk | while | flops 20484 | bytes 63601 | solution.py:61
  337.6 6.2 gather_fusion
  343.8 6.2 gather_fusion
  350.1 6.2 gather_fusion
  356.3 6.2 gather_fusion
  362.5 6.2 gather_fusion
  368.8 6.2 gather_fusion
  375.0 6.2 gather_fusion
  381.3 6.2 gather_fusion
  387.5 6.2 gather_fusion
  393.7 6.2 gather_fusion
  400.0 6.2 gather_fusion
  406.2 6.2 gather_fusion
  412.5 6.2 gather_fusion
  418.7 6.2 gather_fusion
  425.0 4.9 collective-permute-start.11
  435.3 87.3 %while.49 = (s32[]{:T(128)}, u32[1024]{0:T(1024)S(1)}, u32[1024]{0:T(1024)S(1)}, s32[8192]{0:T(1024)S(1)}, s32[]{:T(128)}, /*index=5*/s32[]{:T(128)}, s32[]{:T(128)}, s32[]{}) while((s32[]{:T(128)}, u32[1024]{0:T(1024)S(1)}, u32[1024]{0:T(1024)S(1)}, s32[8192]{0:T(1024)S(1)}, s32[]{:T(128)}, /*index=5*/s32[]{:T(128)}, s32[]{:T(128)}, ...), condition=%wide.region_3.4_spmd.clone, body=%wide.region_2.3_spmd.clone.sunk | while | flops 20484 | bytes 63601 | solution.py:62
  435.3 6.2 gather_fusion.1
  441.5 6.2 gather_fusion.1
  447.8 6.2 gather_fusion.1
  454.0 6.2 gather_fusion.1
  460.2 6.2 gather_fusion.1
  466.5 6.2 gather_fusion.1
  472.7 6.2 gather_fusion.1
  479.0 6.2 gather_fusion.1
  485.2 6.2 gather_fusion.1
  491.4 6.2 gather_fusion.1
  497.7 6.2 gather_fusion.1
  503.9 6.2 gather_fusion.1
  510.1 6.2 gather_fusion.1
  516.4 6.2 gather_fusion.1
  523.2 3.6 fusion.6
  526.9 4.0 fusion.11
  534.8 100.6 %psum.21 = f32[]{:T(128)} all-reduce(f32[]{:T(128)} %get-tuple-element.208), channel_id=1, replica_groups=mesh['rows'=64,'cols'=8] {'rows','cols'}, use_global_device_ids=true, to_apply=%region_6.7 | all-reduce | flops 1 | bytes 8 | tf_op jit(solution)/shard_map/psum | solution.py:77
  637.1 152.3 %all-reduce.1 = (f32[512]{0:T(512)S(1)}, f32[]{:T(128)}) all-reduce(f32[512]{0:T(512)S(1)} %bitcast.25, f32[]{:T(128)} %get-tuple-element.206), channel_id=1, replica_groups=mesh['rows'=64,'cols'=8] {'rows'}, use_global_device_ids=true, to_apply=%region_7.8 | all-reduce | flops 513 | bytes 4104 | tf_op jit(solution)/shard_map/psum | solution.py:78
  790.7 357.4 %all-reduce.4.cloned.1.call-done = f32[512,1,512]{2,1,0:T(1,128)} async-done(((f32[512,1,512]{2,1,0:T(1,128)}), f32[512,1,512]{2,1,0:T(1,128)}) %all-reduce.4.cloned.1.call-update) | async-done | bytes 1048592
  (173 shorter events, 46.3 us)
Async XLA Ops:
  7.2 1140.9 %all-reduce.4.cloned.1.call-start = ((), (), s32[]{:S(2)}) async-start(), calls=%async_computation | async-start | bytes 2097152
  15.9 4.3 copy-start.6
  16.0 50.0 %collective-permute-start = (f32[1024,512]{1,0:T(8,128)S(1)}, f32[1024,512]{1,0:T(8,128)}, u32[]{:S(2)}, u32[]{:S(2)}) collective-permute-start(f32[1024,512]{1,0:T(8,128)S(1)} %bitcast.22), channel_id=1, source_target_pairs={{0,8},{8,0},{16,24},{24,16},{32,40},{40,32},{48,56},{56,48},{64,72... | collective-permute-start | bytes 6291464 | tf_op jit(solution)/shard_map/ppermute | solution.py:20
  68.7 2.4 copy-start.5
  68.7 48.8 %collective-permute-start.1 = (f32[1024,512]{1,0:T(8,128)S(1)}, f32[1024,512]{1,0:T(8,128)}, u32[]{:S(2)}, u32[]{:S(2)}) collective-permute-start(f32[1024,512]{1,0:T(8,128)S(1)} %add_select_fusion.5), channel_id=1, source_target_pairs={{0,16},{16,0},{8,24},{24,8},{32,48},{48,32},{40,56},{56,40},{64,80... | collective-permute-start | bytes 6291464 | tf_op jit(solution)/shard_map/ppermute | solution.py:20
  120.2 4.5 copy-start.4
  120.2 92.8 %collective-permute-start.2 = (f32[1024,512]{1,0:T(8,128)S(1)}, f32[1024,512]{1,0:T(8,128)}, u32[]{:S(2)}, u32[]{:S(2)}) collective-permute-start(f32[1024,512]{1,0:T(8,128)S(1)} %add_select_fusion.4), channel_id=1, source_target_pairs={{0,32},{32,0},{8,40},{40,8},{16,48},{48,16},{24,56},{56,24},{64,96... | collective-permute-start | bytes 6291464 | tf_op jit(solution)/shard_map/ppermute | solution.py:20
  124.8 96.1 %copy-start.7 = (s32[1024]{0:T(1024)S(1)}, s32[1024]{0:T(1024)}, u32[]{:S(2)}) copy-start(s32[1024]{0:T(1024)} %param.9) | copy-start | bytes 12292
  124.8 96.1 %copy-start.8 = (f32[1024]{0:T(1024)S(1)}, f32[1024]{0:T(1024)}, u32[]{:S(2)}) copy-start(f32[1024]{0:T(1024)} %param.10) | copy-start | bytes 12292
  215.7 116.6 %copy-start.3 = (f32[1024,512]{1,0:T(8,128)}, f32[1024,512]{1,0:T(8,128)S(1)}, u32[]{:S(2)}) copy-start(f32[1024,512]{1,0:T(8,128)S(1)} %add_select_fusion.3) | copy-start | bytes 6291460
  215.7 116.6 %collective-permute-start.3 = (f32[1024,512]{1,0:T(8,128)S(1)}, f32[1024,512]{1,0:T(8,128)}, u32[]{:S(2)}, u32[]{:S(2)}) collective-permute-start(f32[1024,512]{1,0:T(8,128)S(1)} %add_select_fusion.3), channel_id=1, source_target_pairs={{0,64},{64,0},{8,72},{72,8},{16,80},{80,16},{24,88},{88,24},{32,96... | collective-permute-start | bytes 6291464 | tf_op jit(solution)/shard_map/ppermute | solution.py:20
  221.4 5.5 collective-permute-start.6
  226.9 86.1 %collective-permute-start.7 = (f32[1024]{0:T(1024)S(1)}, f32[1024]{0:T(1024)S(1)}, u32[]{:S(2)}, u32[]{:S(2)}) collective-permute-start(f32[1024]{0:T(1024)S(1)} %add_select_fusion.11), channel_id=1, source_target_pairs={{0,16},{16,0},{8,24},{24,8},{32,48},{48,32},{40,56},{56,40},{64,80... | collective-permute-start | bytes 12296 | tf_op jit(solution)/shard_map/ppermute | solution.py:20
  313.0 6.4 collective-permute-start.8
  319.4 9.4 collective-permute-start.9
  328.8 8.7 copy-start
  328.8 96.1 %collective-permute-start.10 = (f32[1024]{0:T(1024)S(1)}, f32[1024]{0:T(1024)S(1)}, u32[]{:S(2)}, u32[]{:S(2)}) collective-permute-start(f32[1024]{0:T(1024)S(1)} %add_select_fusion.8), channel_id=1, source_target_pairs={{0,128},{128,0},{8,136},{136,8},{16,144},{144,16},{24,152},{152,24... | collective-permute-start | bytes 12296 | tf_op jit(solution)/shard_map/ppermute | solution.py:20
  335.1 2.5 copy-start.2
  335.1 94.8 %collective-permute-start.4 = (f32[1024,512]{1,0:T(8,128)S(1)}, f32[1024,512]{1,0:T(8,128)}, u32[]{:S(2)}, u32[]{:S(2)}) collective-permute-start(f32[1024,512]{1,0:T(8,128)S(1)} %add_select_fusion.2), channel_id=1, source_target_pairs={{0,128},{128,0},{8,136},{136,8},{16,144},{144,16},{24,152},{152,24... | collective-permute-start | bytes 6291464 | tf_op jit(solution)/shard_map/ppermute | solution.py:20
  425.0 97.7 %collective-permute-start.11 = (f32[1024]{0:T(1024)S(1)}, f32[1024]{0:T(1024)S(1)}, u32[]{:S(2)}, u32[]{:S(2)}) collective-permute-start(f32[1024]{0:T(1024)S(1)} %add_select_fusion.7), channel_id=1, source_target_pairs={{0,256},{256,0},{8,264},{264,8},{16,272},{272,16},{24,280},{280,24... | collective-permute-start | bytes 12296 | tf_op jit(solution)/shard_map/ppermute | solution.py:20
  432.6 2.7 copy-start.1
  432.6 90.6 %collective-permute-start.5 = (f32[1024,512]{1,0:T(8,128)S(1)}, f32[1024,512]{1,0:T(8,128)}, u32[]{:S(2)}, u32[]{:S(2)}) collective-permute-start(f32[1024,512]{1,0:T(8,128)S(1)} %add_select_fusion.1), channel_id=1, source_target_pairs={{0,256},{256,0},{8,264},{264,8},{16,272},{272,16},{24,280},{280,24... | collective-permute-start | bytes 6291464 | tf_op jit(solution)/shard_map/ppermute | solution.py:20
Sparse Core Ops, SparseCore 0:
  533.0 615.0 all-reduce.3
where the time goes:
time: 1160 us
  waiting for transfers between devices  628 us (54%)
  blocking collectives  253 us (22%)
  local copies, waits for them, and re-layouts  176 us (15%)
  starting transfers between devices  46.5 us (4%)
  other arithmetic  23.2 us (2%)
  between operations  16.5 us (1%)
  matrix products  11.6 us (1%)
    unnamed x2, waiting for transfers between devices  357 us
    ppermute x12, waiting for transfers between devices, swapped(): return lax.ppermute(block, axis, route)  271 us
    psum x1, blocking collectives, local(): rhs_sum, power = lax.psum((rhs_part, power_part), 'rows')  152 us
    psum x1, blocking collectives, local(): trace_sum = lax.psum(trace_part, ('rows', 'cols'))  101 us
    gather x14, local copies, waits for them, and re-layouts, local(): jnp.searchsorted(picks, global_rows, side='right')  86.1 us
    gather x14, local copies, waits for them, and re-layouts, local(): jnp.searchsorted(picks, global_rows, side='left')  86.1 us
    ppermute x12, starting transfers between devices, swapped(): return lax.ppermute(block, axis, route)  46.4 us
  transfers between devices with their start and end apart: 13, of which 8 were waited for; matrix products, arithmetic and copies ran while one was open for 16% of the time, Pallas kernels for 0%

commit v1 on v0

v1 whole, which is shorter than its diff:
```python
import jax
import jax.numpy as jnp
from jax import lax
from jax.sharding import PartitionSpec as P

D = 4096
BW = 512

epsilon = 1e-06


def sylvester(order, dtype):
    row_ids = lax.broadcasted_iota(jnp.int32, (order, order), 0)
    col_ids = lax.broadcasted_iota(jnp.int32, (order, order), 1)
    common = jnp.bitwise_and(row_ids, col_ids)
    return (1 - 2 * jnp.bitwise_and(lax.population_count(common), 1)).astype(dtype)


def halves(values):
    top = lax.reduce_precision(values, 8, 7)
    rest = values - top
    return top.astype(jnp.bfloat16), rest.astype(jnp.bfloat16)


def thirds(values):
    top = lax.reduce_precision(values, 8, 7)
    rest = values - top
    mid = lax.reduce_precision(rest, 8, 7)
    low = rest - mid
    return tuple(part.astype(jnp.bfloat16) for part in (top, mid, low))


def dot(left, right):
    return jnp.dot(left, right, preferred_element_type=jnp.float32)


def mix(order, values):
    matrix = sylvester(order, jnp.bfloat16)
    return sum(dot(matrix, part) for part in halves(values))


def local(design, signs, response, picks):
    height, width = design.shape
    groups = lax.axis_size("rows")
    position = lax.axis_index("rows")
    share = height // groups
    flips = signs.astype(jnp.float32)

    whole = lax.all_gather(response * flips, "rows", axis=0, tiled=True)
    side = 256
    square = whole.reshape(side, side)
    h_side = sylvester(side, jnp.bfloat16)
    square = sum(dot(h_side, part) for part in thirds(square))
    square = sum(dot(part, h_side) for part in thirds(square))
    answer = square.reshape(groups, groups, share)
    answer = lax.dynamic_slice_in_dim(answer, position, 1, axis=1)[:, 0, :]

    mixed = mix(height, design * flips[:, None])
    mixed = lax.all_to_all(
        mixed.reshape(groups, share, width), "rows", split_axis=0, concat_axis=0, tiled=True
    )
    mixed = mix(groups, mixed.reshape(groups, share * width)).reshape(height, width)

    group_of = picks // height
    inside = picks % height - position * share
    of_group = (lax.iota(jnp.int32, groups)[:, None] == group_of[None, :]).astype(jnp.bfloat16)
    of_local = (inside[:, None] == lax.iota(jnp.int32, share)[None, :]).astype(jnp.bfloat16)
    picked = dot(of_group, of_local)

    picked_answer = picked * answer
    chosen = mixed * picked.reshape(height)[:, None]
    top, rest = halves(chosen)

    def outer(left, right):
        return lax.dot_general(left, right, (((0,), (0,)), ((), ())), preferred_element_type=jnp.float32)

    cross = outer(top, rest)
    gram = outer(top, top) + cross + cross.T
    rhs_part = jnp.sum(chosen * picked_answer.reshape(height)[:, None], axis=0)
    power_part = jnp.sum(picked_answer * picked_answer)
    trace_part = jnp.sum(chosen * chosen)
    trace_sum = lax.psum(trace_part, ("rows", "cols"))

    blocks = gram.reshape(groups, BW // groups, width)
    extra = jnp.stack([rhs_part, jnp.full((width,), power_part)])
    extra = jnp.broadcast_to(extra[None], (groups, 2, width))
    parts = jnp.concatenate([blocks, extra], axis=1)
    parts = lax.all_to_all(parts, "rows", split_axis=0, concat_axis=0, tiled=True)
    sums = jnp.sum(parts, axis=0)

    mean_diag = trace_sum / D + epsilon
    gram_blocks = sums[: BW // groups, None, :] / mean_diag
    samples = picks.shape[0]
    rhs = sums[BW // groups] * jnp.sqrt(jnp.float32(samples)) / jnp.sqrt(mean_diag * sums[BW // groups + 1])
    return (gram_blocks, rhs)


def solution(mesh):
    in_specs = (P("rows", "cols"), P("rows"), P("rows"), P())
    out_specs = (P("rows", "cols", None), P("cols"))
    return jax.shard_map(local, mesh=mesh, in_specs=in_specs, out_specs=out_specs, check_vma=False)
```

time: 1160 us -> 367 us (0.32)
  the two profiles are of different devices: /device:TPU:8 before, /device:TPU:1 now
where the time goes in v1:
time: 367 us; the launch traced here: 365 us
  blocking collectives  313 us (85%)
  starting transfers between devices  17.7 us (5%)
  matrix products  15.4 us (4%)
  local copies, waits for them, and re-layouts  14.7 us (4%)
    all_gather x1, blocking collectives, local(): whole = lax.all_gather(response * flips, 'rows', axis=0, tiled=True)  164 us
    psum x1, blocking collectives, local(): trace_sum = lax.psum(trace_part, ('rows', 'cols'))  149 us
    all_to_all x1, starting transfers between devices, local(): lax.all_to_all(mixed.reshape(groups, share, width), 'rows', split_axis=0,...  13.1 us
    dot_general x11, matrix products, dot(): return jnp.dot(left, right, preferred_element_type=jnp.float32)  11.4 us
  transfers between devices with their start and end apart: 2, of which 0 were waited for; matrix products, arithmetic and copies ran while one was open for 2% of the time, Pallas kernels for 0%

profile of v1, /device:TPU:1, one launch (start us, length us, event | category | flops | bytes accessed | tf_op | source)
XLA Modules:
  0.0 365.5 jit_solution(7511353022532499297)
XLA Ops:
  0.6 0.7 convert_element_type.74
  1.3 3.2 fusion.3
  4.5 2.7 fusion.6
  7.2 13.1 %all-to-all-start = ((f32[64,16,512]{2,1,0:T(8,128)}), f32[64,16,512]{2,1,0:T(8,128)S(1)}, u32[]{:S(2)}, u32[]{:S(2)}) async-start(f32[64,16,512]{2,1,0:T(8,128)} %bitcast.23), calls=%async_computation | async-start | bytes 4194304 | tf_op jit(solution)/shard_map/all_to_all | solution.py:59
  20.3 0.0 copy-done.2
  20.3 0.0 copy-done.3
  20.3 163.9 %all_gather.3 = f32[65536]{0:T(1024)S(1)} all-gather(f32[1024]{0:T(1024)S(1)} %convert_multiply_fusion), channel_id=1, replica_groups=mesh['rows'=64,'cols'=8] {'rows'}, dimensions={0}, use_global_device_ids=true | all-gather | bytes 266240 | tf_op jit(solution)/shard_map/all_gather | solution.py:49
  184.2 0.1 reshape.58
  184.3 0.2 fusion.20
  184.5 0.2 convolution_add_fusion.5
  184.7 0.2 convolution_add_fusion.4
  185.0 0.2 fusion.21
  185.2 0.0 copy-start.1
  185.2 0.2 convolution_add_fusion.3
  185.4 0.2 convolution_add_fusion.2
  185.7 2.0 reshape.59
  187.6 1.0 constant_dynamic-slice_fusion
  188.6 0.1 copy.22
  188.7 0.0 copy-done.1
  188.7 1.1 multiply_reduce_fusion.2
  189.8 0.1 copy.23
  189.9 0.1 mul.118
  190.0 0.1 copy.19
  190.1 0.1 mul.111
  190.1 0.2 mul.108
  190.3 2.5 copy.25
  192.8 0.0 all-to-all-done
  192.8 1.2 copy.24
  194.0 0.0 copy-start
  194.0 0.4 fusion.11
  194.5 1.2 copy-done
  195.6 2.7 multiply_reduce_fusion
  198.4 1.3 convert_element_type.82
  199.7 0.5 convert_element_type.80
  200.2 2.0 fusion.47
  202.1 1.3 copy.20
  203.5 2.0 fusion.8
  205.4 1.8 reshape.57
  207.2 0.4 multiply_reduce_fusion.1
  207.6 0.7 stack.7
  208.2 0.1 broadcast_in_dim.2
  208.3 1.6 pad_maximum_fusion
  209.9 4.7 %all-to-all-start.1 = ((f32[64,10,512]{2,1,0:T(8,128)}), f32[64,10,512]{2,1,0:T(8,128)S(1)}, u32[]{:S(2)}, u32[]{:S(2)}) async-start(f32[64,10,512]{2,1,0:T(8,128)} %pad_maximum_fusion), calls=%async_computation.1 | async-start | bytes 4194304 | tf_op jit(solution)/shard_map/all_to_all | solution.py:88
  214.6 148.8 %psum.7 = f32[]{:T(128)} all-reduce(f32[]{:T(128)} %get-tuple-element.4), channel_id=1, replica_groups=mesh['rows'=64,'cols'=8] {'rows','cols'}, use_global_device_ids=true, to_apply=%region_4.5 | all-reduce | flops 1 | bytes 8 | tf_op jit(solution)/shard_map/psum | solution.py:82
  364.1 0.0 all-to-all-done.1
  364.1 0.2 reduce_sum.38
  364.3 0.6 fusion.26
  364.9 0.6 div.36
  (7 shorter events, 0.1 us)
Async XLA Ops:
  1.3 3.2 copy-start.4
  7.2 13.1 %copy-start.2 = (s32[1024]{0:T(1024)S(1)}, s32[1024]{0:T(1024)}, u32[]{:S(2)}) copy-start(s32[1024]{0:T(1024)} %param.5) | copy-start | bytes 12292
  7.2 13.1 %copy-start.3 = (f32[1024]{0:T(1024)S(1)}, f32[1024]{0:T(1024)}, u32[]{:S(2)}) copy-start(f32[1024]{0:T(1024)} %param.6) | copy-start | bytes 12292
  7.2 185.6 %all-to-all-start = ((f32[64,16,512]{2,1,0:T(8,128)}), f32[64,16,512]{2,1,0:T(8,128)S(1)}, u32[]{:S(2)}, u32[]{:S(2)}) async-start(f32[64,16,512]{2,1,0:T(8,128)} %bitcast.23), calls=%async_computation | async-start | bytes 4194304 | tf_op jit(solution)/shard_map/all_to_all | solution.py:59
  185.2 3.5 copy-start.1
  194.0 1.6 copy-start
  209.9 154.2 %all-to-all-start.1 = ((f32[64,10,512]{2,1,0:T(8,128)}), f32[64,10,512]{2,1,0:T(8,128)S(1)}, u32[]{:S(2)}, u32[]{:S(2)}) async-start(f32[64,10,512]{2,1,0:T(8,128)} %pad_maximum_fusion), calls=%async_computation.1 | async-start | bytes 4194304 | tf_op jit(solution)/shard_map/all_to_all | solution.py:88

commit v2 on v1

v2 whole, which is shorter than its diff:
```python
import functools

import jax
import jax.numpy as jnp
from jax import lax
from jax.experimental import pallas as pl
from jax.experimental.pallas import tpu as pltpu
from jax.sharding import PartitionSpec as P

D = 4096
BW = 512

epsilon = 1e-06


def sylvester(order, dtype):
    row_ids = lax.broadcasted_iota(jnp.int32, (order, order), 0)
    col_ids = lax.broadcasted_iota(jnp.int32, (order, order), 1)
    common = jnp.bitwise_and(row_ids, col_ids)
    return (1 - 2 * jnp.bitwise_and(lax.population_count(common), 1)).astype(dtype)


def halves(values):
    top = lax.reduce_precision(values, 8, 7)
    rest = values - top
    return top.astype(jnp.bfloat16), rest.astype(jnp.bfloat16)


def dot(left, right):
    return jnp.dot(left, right, preferred_element_type=jnp.float32)


def mix(order, values):
    matrix = sylvester(order, jnp.bfloat16)
    return sum(dot(matrix, part) for part in halves(values))


MESH = pl.DeviceIdType.MESH
VMEM = pltpu.VMEM
LANES = 128


def peer(groups, k):
    me = lax.axis_index("rows")
    x = lax.rem(me // 16 + k // 16, groups // 16)
    y = lax.rem(lax.rem(me // 2, 8) + lax.rem(k, 8), 8)
    z = lax.rem(lax.rem(me, 2) + lax.rem(k // 8, 2), 2)
    return x * 16 + y * 2 + z


def each_peer(groups, action):
    def step(k, carry):
        action(peer(groups, k))
        return carry

    lax.fori_loop(1, groups, step, 0)


def to_row(source, landing, sends, receives, slot, there):
    return pltpu.make_async_remote_copy(
        src_ref=source,
        dst_ref=landing.at[slot],
        send_sem=sends.at[there],
        recv_sem=receives.at[slot],
        device_id={"rows": there},
        device_id_type=MESH,
    )


def greet_rows(groups):
    barrier = pltpu.get_barrier_semaphore()
    each_peer(
        groups,
        lambda there: pl.semaphore_signal(barrier, inc=1, device_id={"rows": there}, device_id_type=MESH),
    )
    return barrier


def trade_kernel(groups, mixed, answer, mixed_out, answer_out, sends, receives, answer_sends, answer_receives, own):
    me = lax.axis_index("rows")
    pl.semaphore_wait(greet_rows(groups), groups - 1)

    def start(there):
        to_row(mixed.at[there], mixed_out, sends, receives, me, there).start()
        to_row(answer.at[there], answer_out, answer_sends, answer_receives, me, there).start()

    def finish(there):
        to_row(mixed.at[there], mixed_out, sends, receives, there, there).wait()
        to_row(answer.at[there], answer_out, answer_sends, answer_receives, there, there).wait()

    each_peer(groups, start)
    keep = pltpu.make_async_copy(mixed.at[me], mixed_out.at[me], own.at[0])
    keep_answer = pltpu.make_async_copy(answer.at[me], answer_out.at[me], own.at[1])
    keep.start()
    keep_answer.start()
    keep.wait()
    keep_answer.wait()
    each_peer(groups, finish)


def trade(mixed, answer):
    groups = mixed.shape[0]
    return pl.pallas_call(
        functools.partial(trade_kernel, groups),
        out_shape=[
            jax.ShapeDtypeStruct(mixed.shape, jnp.float32),
            jax.ShapeDtypeStruct(answer.shape, jnp.float32),
        ],
        in_specs=[pl.BlockSpec(memory_space=VMEM)] * 2,
        out_specs=[pl.BlockSpec(memory_space=VMEM)] * 2,
        scratch_shapes=[pltpu.SemaphoreType.DMA((groups,))] * 4 + [pltpu.SemaphoreType.DMA((2,))],
        compiler_params=pltpu.CompilerParams(collective_id=0, has_side_effects=True),
    )(mixed, answer)


def finish_kernel(
    groups, columns, samples, gram, small, gram_out, rhs_out,
    land, land_small, land_total, total,
    sends, receives, small_sends, small_receives, total_sends, total_receives, own,
):
    me = lax.axis_index("rows")
    column = lax.axis_index("cols")
    barrier = greet_rows(groups)
    for k in range(1, columns):
        there = lax.rem(column + k, columns)
        pl.semaphore_signal(barrier, inc=1, device_id={"cols": there}, device_id_type=MESH)
    pl.semaphore_wait(barrier, groups + columns - 2)

    each_peer(groups, lambda there: to_row(small, land_small, small_sends, small_receives, me, there).start())
    each_peer(groups, lambda there: to_row(gram.at[there], land, sends, receives, me, there).start())
    keep = pltpu.make_async_copy(gram.at[me], land.at[me], own.at[0])
    keep_small = pltpu.make_async_copy(small, land_small.at[me], own.at[1])
    keep.start()
    keep_small.start()
    keep.wait()
    keep_small.wait()
    each_peer(groups, lambda there: to_row(small, land_small, small_sends, small_receives, there, there).wait())
    total[...] = jnp.sum(land_small[...], axis=0)

    def to_column(slot, there):
        return pltpu.make_async_remote_copy(
            src_ref=total,
            dst_ref=land_total.at[slot],
            send_sem=total_sends.at[there],
            recv_sem=total_receives.at[slot],
            device_id={"cols": there},
            device_id_type=MESH,
        )

    for k in range(1, columns):
        to_column(column, lax.rem(column + k, columns)).start()
    each_peer(groups, lambda there: to_row(gram.at[there], land, sends, receives, there, there).wait())
    sums = jnp.sum(land[...], axis=0)
    mine = total[...]
    trace = mine[4:5, :]
    for k in range(1, columns):
        there = lax.rem(column + k, columns)
        to_column(there, there).wait()
        trace = trace + land_total[there][4:5, :]
    mean_diag = trace / D + epsilon
    for j in range(BW // LANES):
        gram_out[:, j * LANES:(j + 1) * LANES] = sums[:, j * LANES:(j + 1) * LANES] / mean_diag
    rhs_out[...] = mine * jnp.sqrt(jnp.float32(samples)) / jnp.sqrt(mean_diag * mine[5:6, :])


def finish(gram, small, columns, samples):
    groups, height, width = gram.shape
    return pl.pallas_call(
        functools.partial(finish_kernel, groups, columns, samples),
        out_shape=[
            jax.ShapeDtypeStruct((height, width), jnp.float32),
            jax.ShapeDtypeStruct(small.shape, jnp.float32),
        ],
        in_specs=[pl.BlockSpec(memory_space=VMEM)] * 2,
        out_specs=[pl.BlockSpec(memory_space=VMEM)] * 2,
        scratch_shapes=[
            VMEM(gram.shape, jnp.float32),
            VMEM((groups,) + small.shape, jnp.float32),
            VMEM((columns,) + small.shape, jnp.float32),
            VMEM(small.shape, jnp.float32),
        ]
        + [pltpu.SemaphoreType.DMA((groups,))] * 4
        + [pltpu.SemaphoreType.DMA((columns,))] * 2
        + [pltpu.SemaphoreType.DMA((2,))],
        compiler_params=pltpu.CompilerParams(collective_id=1, has_side_effects=True),
    )(gram, small)


def local(design, signs, response, picks):
    height, width = design.shape
    groups = lax.axis_size("rows")
    position = lax.axis_index("rows")
    share = height // groups
    flips = signs.astype(jnp.float32)

    exact = lax.Precision.HIGHEST
    h_32 = sylvester(32, jnp.float32)
    answer = jnp.dot(h_32, (response * flips).reshape(32, 32), precision=exact)
    answer = jnp.dot(answer, h_32, precision=exact).reshape(groups, 1, share)
    answer = jnp.pad(answer, ((0, 0), (0, 0), (0, LANES - share)))

    mixed = mix(height, design * flips[:, None])
    mixed, answer = trade(mixed.reshape(groups, share, width), answer)
    mixed = mix(groups, mixed.reshape(groups, share * width)).reshape(height, width)
    answer = jnp.dot(sylvester(groups, jnp.float32), answer[:, 0, :share], precision=exact)

    group_of = picks // height
    inside = picks % height - position * share
    of_group = (lax.iota(jnp.int32, groups)[:, None] == group_of[None, :]).astype(jnp.bfloat16)
    of_local = (inside[:, None] == lax.iota(jnp.int32, share)[None, :]).astype(jnp.bfloat16)
    picked = dot(of_group, of_local)

    picked_answer = picked * answer
    chosen = mixed * picked.reshape(height)[:, None]
    top, rest = halves(chosen)

    def outer(left, right):
        return lax.dot_general(left, right, (((0,), (0,)), ((), ())), preferred_element_type=jnp.float32)

    cross = outer(top, rest)
    gram = outer(top, top) + cross + cross.T
    rhs_part = jnp.sum(chosen * picked_answer.reshape(height)[:, None], axis=0)
    power_part = jnp.sum(picked_answer * picked_answer)
    trace_part = jnp.sum(chosen * chosen)
    small = jnp.concatenate([
        rhs_part.reshape(BW // LANES, LANES),
        jnp.full((1, LANES), trace_part),
        jnp.full((1, LANES), power_part),
        jnp.zeros((2, LANES), jnp.float32),
    ])
    gram_rows, small = finish(
        gram.reshape(groups, BW // groups, width), small, lax.axis_size("cols"), picks.shape[0]
    )
    return (gram_rows[:, None, :], small[: BW // LANES].reshape(BW))


def solution(mesh):
    in_specs = (P("rows", "cols"), P("rows"), P("rows"), P())
    out_specs = (P("rows", "cols", None), P("cols"))
    return jax.shard_map(local, mesh=mesh, in_specs=in_specs, out_specs=out_specs, check_vma=False)
```

time: 367 us -> 150 us (0.41)
  blocking collectives: 313 us -> 0 us
  Pallas kernels: 0 us -> 115 us
  starting transfers between devices: 17.7 us -> 0 us
    all_gather x1 -> x0, blocking collectives: 164 us -> none  [local(): whole = lax.all_gather(response * flips, 'rows', axis=0, tiled=True)]
    psum x1 -> x0, blocking collectives: 149 us -> none  [local(): trace_sum = lax.psum(trace_part, ('rows', 'cols'))]
    pallas_call x0 -> x2, Pallas kernels: none -> 115 us  [the longest x1 64.8 us: trade(): pl.pallas_call(functools.partial(trade_kernel, groups), out_shape=[jax.Sh...]
    all_to_all x2 -> x0, starting transfers between devices: 17.7 us -> none  [the longest x1 13.1 us: local(): lax.all_to_all(mixed.reshape(groups, share, width), 'rows', split_axis=0,...]
    dot_general x11 -> x5, matrix products: 11.4 us -> 8.1 us  [dot(): return jnp.dot(left, right, preferred_element_type=jnp.float32)]
    unnamed x12 -> x9, local copies, waits for them, and re-layouts: 4.87 us -> 7.89 us
  transfers between devices with their start and end apart: 2 -> 0, of which waited for: 0 -> 0; matrix products, arithmetic and copies ran while one was open for 2% -> 0% of each run, Pallas kernels for 0% -> 0%
where the time goes in v2:
time: 150 us; the launch traced here: 149 us
  Pallas kernels  115 us (77%)
  local copies, waits for them, and re-layouts  16.9 us (11%)
  matrix products  12.9 us (9%)
  other arithmetic  3.21 us (2%)
    pallas_call x1, Pallas kernels, trade(): pl.pallas_call(functools.partial(trade_kernel, groups), out_shape=[jax.Sh...  64.8 us
    pallas_call x1, Pallas kernels, finish(): pl.pallas_call(functools.partial(finish_kernel, groups, columns, samples)...  50.5 us
    dot_general x5, matrix products, dot(): return jnp.dot(left, right, preferred_element_type=jnp.float32)  8.1 us
    unnamed x9, local copies, waits for them, and re-layouts  7.89 us
    dot_general x2, matrix products, outer(): lax.dot_general(left, right, (((0,), (0,)), ((), ())), preferred_element_...  3.68 us

profile of v2, /device:TPU:1, one launch (start us, length us, event | category | flops | bytes accessed | tf_op | source)
XLA Modules:
  0.0 149.0 jit_solution(15185970295710647838)
XLA Ops:
  0.6 0.1 pad.8.clone
  0.7 0.7 convert_element_type.53
  1.4 0.7 convert_multiply_fusion
  2.1 0.1 reshape.53
  2.2 0.1 fusion.23
  2.3 0.2 fusion.21
  2.5 0.1 reshape.54
  2.6 0.6 pad.4.answer
  3.2 0.8 fusion.16
  4.0 0.5 fusion.5
  4.5 0.1 copy.16
  4.6 0.1 mul.91
  4.6 0.2 mul.88
  4.9 0.0 copy-start.2
  4.9 2.5 %copy.22 = f32[8,8,16,512]{3,1,2,0:T(8,128)} copy(f32[8,8,16,512]{3,2,1,0:T(8,128)S(1)} %bitcast.27) | data formatting | bytes 4194304
  7.4 0.0 copy-done.2
  7.4 1.5 fusion.3
  8.9 2.7 %fusion.6 = f32[1024,512]{1,0:T(8,128)} fusion(f32[1024,512]{1,0:T(8,128)S(1)} %fusion.3, f32[1024,512]{1,0:T(8,128)S(1)} %copy-done.2, f32[1024]{0:T(1024)S(1)} %convert_element_type.53), kind=kOutput, calls=%fused_computation.17 | convolution fusion | flops 1082130432 | bytes 6295552 | tf_op jit(solution)/shard_map/dot_general | solution.py:30
  11.6 64.8 %shard_map.59 = (f32[64,16,512]{2,1,0:T(8,128)}, f32[64,1,128]{2,1,0:T(1,128)}) custom-call(f32[64,16,512]{2,1,0:T(8,128)} %bitcast.29, f32[64,1,128]{2,1,0:T(1,128)} %pad.4.answer), custom_call_target="tpu_custom_call" | custom-call | tf_op jit(solution)/shard_map/pallas_call | solution.py:103
  76.3 0.0 copy-start.1
  76.3 2.8 %copy.21 = f32[8,8,16,512]{3,1,2,0:T(8,128)S(1)} copy(f32[8,8,16,512]{3,2,1,0:T(8,128)} %bitcast.30) | data formatting | bytes 4194304
  79.1 0.0 copy-done.1
  79.2 0.8 multiply_reduce_fusion.2
  80.0 0.7 pad.7.clone
  80.7 0.1 copy.19
  80.8 0.1 mul.95
  80.9 0.0 copy-start
  80.9 0.4 fusion.11
  81.3 1.2 copy-done
  82.5 3.1 %multiply_reduce_fusion = (f32[]{:T(128)}, bf16[64,8192]{1,0:T(8,128)(2,1)}, bf16[64,8192]{1,0:T(8,128)(2,1)S(1)}, f32[64,8192]{1,0:T(8,128)}) fusion(f32[64,8192]{1,0:T(8,128)S(1)} %bitcast.28, f32[64,8192]{1,0:T(8,128)S(1)} %fusion.11, f32[64,8192]{1,0:T(8,128)S(1)} %bitcast.26), kind=kOutput, calls=%fused_computation.11 | convolution fusion | flops 72900608 | bytes 10485764 | tf_op jit(solution)/shard_map/dot_general | solution.py:30
  85.5 2.3 %convert_element_type.62 = bf16[1024,512]{1,0:T(8,128)(2,1)} reshape(bf16[64,8192]{1,0:T(8,128)(2,1)} %get-tuple-element.17) | data formatting | bytes 2097152 | tf_op jit(solution)/shard_map/convert_element_type | solution.py:26
  87.9 0.7 pad.6.clone
  88.6 0.5 convert_element_type.60
  89.1 2.0 %fusion.47 = f32[512,512]{1,0:T(8,128)S(1)} fusion(bf16[1024,512]{1,0:T(8,128)(2,1)S(1)} %convert_element_type.60, bf16[1024,512]{1,0:T(8,128)(2,1)} %convert_element_type.62), kind=kOutput, calls=%fused_computation.69 | convolution fusion | flops 536870912 | bytes 3145728 | tf_op jit(solution)/shard_map/dot_general | solution.py:218
  91.1 0.3 copy.17
  91.4 1.7 %fusion.8.gram = f32[64,8,512]{2,1,0:T(8,128)} fusion(f32[512,512]{1,0:T(8,128)S(1)} %fusion.47, bf16[1024,512]{1,0:T(8,128)(2,1)S(1)} %convert_element_type.60, f32[512,512]{0,1:T(8,128)S(1)} %copy.17), kind=kOutput, calls=%fused_computation.20 | convolution fusion | flops 537395200 | bytes 4194304 | tf_op jit(solution)/shard_map/dot_general | solution.py:218
  93.1 1.7 %reshape.57 = f32[1024,512]{1,0:T(8,128)S(1)} reshape(f32[64,8192]{1,0:T(8,128)} %get-tuple-element.21) | data formatting | bytes 4194304 | tf_op jit(solution)/shard_map/reshape | solution.py:204
  94.9 0.3 multiply_reduce_fusion.1
  95.2 0.7 maximum_maximum_fusion.small
  95.9 50.5 %shard_map.60 = (f32[8,512]{1,0:T(8,128)}, f32[8,128]{1,0:T(8,128)}) custom-call(f32[64,8,512]{2,1,0:T(8,128)} %fusion.8.gram, f32[8,128]{1,0:T(8,128)} %maximum_maximum_fusion.small), custom_call_target="tpu_custom_call" | custom-call | tf_op jit(solution)/shard_map/pallas_call | solution.py:168
  146.4 1.3 copy.20
  147.7 1.2 slice_bitcast_fusion
  (1 shorter events, 0.0 us)
Async XLA Ops:
  4.9 2.6 %copy-start.2 = (f32[1024,512]{1,0:T(8,128)S(1)}, f32[1024,512]{1,0:T(8,128)}, u32[]{:S(2)}) copy-start(f32[1024,512]{1,0:T(8,128)} %param.4) | copy-start | bytes 6291460
  76.3 2.8 %copy-start.1 = (f32[64,1,128]{2,1,0:T(1,128)S(1)}, f32[64,1,128]{2,1,0:T(1,128)}, u32[]{:S(2)}) copy-start(f32[64,1,128]{2,1,0:T(1,128)} %get-tuple-element.7) | copy-start | bytes 98308
  80.9 1.6 %copy-start = (f32[8,8,16,512]{3,1,2,0:T(8,128)S(1)}, f32[8,8,16,512]{3,1,2,0:T(8,128)}, u32[]{:S(2)}) copy-start(f32[8,8,16,512]{3,1,2,0:T(8,128)} %copy.22) | copy-start | bytes 6291460

commit v3 on v2

v3 whole, which is shorter than its diff:
```python
import functools

import jax
import jax.numpy as jnp
from jax import lax
from jax.experimental import pallas as pl
from jax.experimental.pallas import tpu as pltpu
from jax.sharding import PartitionSpec as P

D = 4096
BW = 512

epsilon = 1e-06


def sylvester(order, dtype):
    row_ids = lax.broadcasted_iota(jnp.int32, (order, order), 0)
    col_ids = lax.broadcasted_iota(jnp.int32, (order, order), 1)
    common = jnp.bitwise_and(row_ids, col_ids)
    return (1 - 2 * jnp.bitwise_and(lax.population_count(common), 1)).astype(dtype)


def halves(values):
    top = values.astype(jnp.bfloat16)
    return top, (values - top.astype(jnp.float32)).astype(jnp.bfloat16)


def dot(left, right):
    return jnp.dot(left, right, preferred_element_type=jnp.float32)


def butterfly(values):
    apart = 1
    while apart < len(values):
        values = [
            values[i ^ apart] - values[i] if i & apart else values[i] + values[i ^ apart]
            for i in range(len(values))
        ]
        apart *= 2
    return values


MESH = pl.DeviceIdType.MESH
VMEM = pltpu.VMEM
LANES = 128


def peer(groups, k):
    me = lax.axis_index("rows")
    x = lax.rem(me // 16 + k // 16, groups // 16)
    y = lax.rem(lax.rem(me // 2, 8) + lax.rem(k, 8), 8)
    z = lax.rem(lax.rem(me, 2) + lax.rem(k // 8, 2), 2)
    return x * 16 + y * 2 + z


def each_peer(groups, action):
    def step(k, carry):
        action(peer(groups, k))
        return carry

    lax.fori_loop(1, groups, step, 0)


def to_row(source, landing, sends, receives, slot, there):
    return pltpu.make_async_remote_copy(
        src_ref=source,
        dst_ref=landing.at[slot],
        send_sem=sends.at[there],
        recv_sem=receives.at[slot],
        device_id={"rows": there},
        device_id_type=MESH,
    )


def greet_rows(groups):
    barrier = pltpu.get_barrier_semaphore()
    each_peer(
        groups,
        lambda there: pl.semaphore_signal(barrier, inc=1, device_id={"rows": there}, device_id_type=MESH),
    )
    return barrier


def trade_kernel(groups, mixed, answer, mixed_out, answer_out, sends, receives, answer_sends, answer_receives, own):
    me = lax.axis_index("rows")
    pl.semaphore_wait(greet_rows(groups), groups - 1)

    def start(there):
        to_row(mixed.at[there], mixed_out, sends, receives, me, there).start()
        to_row(answer.at[there // 8], answer_out, answer_sends, answer_receives, me, there).start()

    def finish(there):
        to_row(mixed.at[there], mixed_out, sends, receives, there, there).wait()
        to_row(answer.at[there // 8], answer_out, answer_sends, answer_receives, there, there).wait()

    each_peer(groups, start)
    keep = pltpu.make_async_copy(mixed.at[me], mixed_out.at[me], own.at[0])
    keep_answer = pltpu.make_async_copy(answer.at[me // 8], answer_out.at[me], own.at[1])
    keep.start()
    keep_answer.start()
    keep.wait()
    keep_answer.wait()
    each_peer(groups, finish)


def trade(mixed, answer):
    groups = mixed.shape[0]
    return pl.pallas_call(
        functools.partial(trade_kernel, groups),
        out_shape=[
            jax.ShapeDtypeStruct(mixed.shape, jnp.float32),
            jax.ShapeDtypeStruct((groups, 1, LANES), jnp.float32),
        ],
        in_specs=[pl.BlockSpec(memory_space=VMEM)] * 2,
        out_specs=[pl.BlockSpec(memory_space=VMEM)] * 2,
        scratch_shapes=[pltpu.SemaphoreType.DMA((groups,))] * 4 + [pltpu.SemaphoreType.DMA((2,))],
        compiler_params=pltpu.CompilerParams(collective_id=0, has_side_effects=True),
    )(mixed, answer)


def mix_kernel(design, signs, response, mixed, answer):
    height, width = design.shape
    blocks = height // LANES
    h_lanes = sylvester(LANES, jnp.float32)
    flips = signs[...].astype(jnp.float32)
    for b in range(blocks):
        top, rest = halves(design[b * LANES:(b + 1) * LANES, :])
        matrix = (h_lanes * flips[b:b + 1, :]).astype(jnp.bfloat16)
        part = dot(matrix, top) + dot(matrix, rest)
        mixed[b * 8:(b + 1) * 8] = part.reshape(8, LANES // 8, width)

    def level(i, carry):
        row = lax.rem(i, 2) * 8
        values = butterfly([mixed[b * 8 + i // 2, pl.ds(row, 8), :] for b in range(blocks)])
        for b in range(blocks):
            mixed[b * 8 + i // 2, pl.ds(row, 8), :] = values[b]
        return carry

    lax.fori_loop(0, LANES // 8, level, 0)
    folded = jnp.dot(response[...] * flips, h_lanes, precision=lax.Precision.HIGHEST, preferred_element_type=jnp.float32)
    rows = butterfly([folded[b:b + 1, :] for b in range(blocks)])
    for b in range(blocks):
        answer[b] = rows[b]


def local_mix(design, signs, response):
    height, width = design.shape
    blocks = height // LANES
    return pl.pallas_call(
        mix_kernel,
        out_shape=[
            jax.ShapeDtypeStruct((64, height // 64, width), jnp.float32),
            jax.ShapeDtypeStruct((blocks, 1, LANES), jnp.float32),
        ],
        in_specs=[pl.BlockSpec(memory_space=VMEM)] * 3,
        out_specs=[pl.BlockSpec(memory_space=VMEM)] * 2,
    )(design, signs.reshape(blocks, LANES), response.reshape(blocks, LANES))


def gram_kernel(mixed, answer, picks, gram, small, held):
    groups, share, width = mixed.shape
    height = groups * share
    position = lax.axis_index("rows")

    def first(i, carry):
        row = lax.rem(i, 2) * 8
        values = butterfly([mixed[i // 2 * 8 + b, pl.ds(row, 8), :] for b in range(8)])
        for b in range(8):
            held[i // 2 * 8 + b, pl.ds(row, 8), :] = values[b]
        return carry

    def second(i, carry):
        row = lax.rem(i, 2) * 8
        values = butterfly([held[b * 8 + i // 2, pl.ds(row, 8), :] for b in range(8)])
        for b in range(8):
            held[b * 8 + i // 2, pl.ds(row, 8), :] = values[b]
        return carry

    lax.fori_loop(0, 16, first, 0)
    lax.fori_loop(0, 16, second, 0)
    mixed_answer = jnp.dot(
        sylvester(groups, jnp.float32), answer[:, 0, :],
        precision=lax.Precision.HIGHEST, preferred_element_type=jnp.float32,
    )
    wanted = picks[...]
    group_of = jnp.right_shift(wanted, 10)
    inside = jnp.bitwise_and(wanted, height - 1) - position * share
    samples = wanted.shape[1]
    of_group = (lax.broadcasted_iota(jnp.int32, (groups, samples), 0) == group_of).astype(jnp.float32)
    of_local = (lax.broadcasted_iota(jnp.int32, (LANES, samples), 0) == inside).astype(jnp.float32)
    picked = lax.dot_general(
        of_group.astype(jnp.bfloat16), of_local[:share].astype(jnp.bfloat16), (((1,), (1,)), ((), ())),
        preferred_element_type=jnp.float32,
    )
    lane = lax.broadcasted_iota(jnp.int32, (groups, share, share), 2)
    local_row = lax.broadcasted_iota(jnp.int32, (groups, share, share), 1)
    picked_rows = jnp.sum(jnp.where(lane == local_row, picked[:, None, :], 0.0), axis=2, keepdims=True)
    lane = lax.broadcasted_iota(jnp.int32, (groups, share, LANES), 2)
    local_row = lax.broadcasted_iota(jnp.int32, (groups, share, LANES), 1) + lax.rem(position, 8) * share
    answer_rows = jnp.sum(jnp.where(lane == local_row, mixed_answer[:, None, :], 0.0), axis=2, keepdims=True)
    picked_rows = picked_rows.reshape(height, 1)
    answer_rows = answer_rows.reshape(height, 1) * picked_rows

    chosen = held[...].reshape(height, width) * picked_rows
    top, rest = halves(chosen)

    def outer(left, right):
        return lax.dot_general(left, right, (((0,), (0,)), ((), ())), preferred_element_type=jnp.float32)

    total = outer(top, top) + outer(top, rest) + outer(rest, top)
    half = width // 2
    for h in range(2):
        gram[h] = total[:, h * half:(h + 1) * half].reshape(gram.shape[1:])
    rhs = jnp.sum(chosen * answer_rows, axis=0, keepdims=True)
    trace = jnp.sum(jnp.sum(chosen * chosen, axis=0, keepdims=True), axis=1, keepdims=True)
    power = jnp.sum(answer_rows * answer_rows, axis=0, keepdims=True)
    for j in range(width // LANES):
        small[j:j + 1, :] = rhs[:, j * LANES:(j + 1) * LANES]
    small[4:5, :] = jnp.broadcast_to(trace, (1, LANES))
    small[5:6, :] = jnp.broadcast_to(power, (1, LANES))
    small[6:8, :] = jnp.zeros((2, LANES), jnp.float32)


def local_gram(mixed, answer, picks):
    groups, share, width = mixed.shape
    return pl.pallas_call(
        gram_kernel,
        out_shape=[
            jax.ShapeDtypeStruct((2, groups // 16, 8, 2, width // groups, width // 2), jnp.float32),
            jax.ShapeDtypeStruct((8, LANES), jnp.float32),
        ],
        in_specs=[pl.BlockSpec(memory_space=VMEM)] * 3,
        out_specs=[pl.BlockSpec(memory_space=VMEM)] * 2,
        scratch_shapes=[VMEM(mixed.shape, jnp.float32)],
        compiler_params=pltpu.CompilerParams(vmem_limit_bytes=60 * 2**20),
    )(mixed, answer, picks.reshape(1, -1))


def finish_kernel(
    columns, samples, gram, small, gram_out, rhs_out,
    a_first, a_first_sum, a_second, a_second_sum, a_third,
    b_first, b_first_sum, b_second, b_second_sum, b_third,
    s_first, s_first_sum, s_second, s_second_sum, s_third,
    sends, receives,
):
    me = lax.axis_index("rows")
    column = lax.axis_index("cols")
    along_x = gram.shape[1]
    x = me // 16
    y = lax.rem(me // 2, 8)
    z = lax.rem(me, 2)
    other_z = 1 - z

    def row_at(kx, ky, kz):
        return lax.rem(x + kx, along_x) * 16 + lax.rem(y + ky, 8) * 2 + lax.rem(z + kz, 2)

    plane = [(kx, kz) for kz in range(2) for kx in range(along_x) if kx or kz]
    plane_rows = [row_at(kx, 0, kz) for kx, kz in plane]
    y_rows = [row_at(0, ky, 0) for ky in range(1, 8)]
    others = [lax.rem(column + k, columns) for k in range(1, columns)]

    barrier = pltpu.get_barrier_semaphore()
    for there in plane_rows + y_rows:
        pl.semaphore_signal(barrier, inc=1, device_id={"rows": there}, device_id_type=MESH)
    for there in others:
        pl.semaphore_signal(barrier, inc=1, device_id={"cols": there}, device_id_type=MESH)
    pl.semaphore_wait(barrier, len(plane_rows) + len(y_rows) + len(others))

    used = []

    def send(source, landing, **there):
        index = len(used)
        used.append(index)
        copy = pltpu.make_async_remote_copy(
            src_ref=source,
            dst_ref=landing,
            send_sem=sends.at[index],
            recv_sem=receives.at[index],
            device_id=there,
            device_id_type=MESH,
        )
        copy.start()
        return copy

    def wait(copies):
        for copy in copies:
            copy.wait()

    s1 = [send(small, s_first.at[k], rows=there) for k, there in enumerate(plane_rows)]
    b1 = [send(gram.at[1, :, :, other_z], b_first, rows=row_at(0, 0, 1))]
    a1 = [
        send(gram.at[0, lax.rem(x + k, along_x)], a_first.at[k - 1], rows=row_at(k, 0, 0))
        for k in (2, 1, 3)
    ]
    wait(s1)
    s_first_sum[...] = small[...] + jnp.sum(s_first[...], axis=0)
    s2 = [send(s_first_sum, s_second.at[k], rows=there) for k, there in enumerate(y_rows)]
    wait(b1)
    b_first_sum[...] = gram[1, :, :, z] + b_first[...]
    b2 = [
        send(b_first_sum.at[lax.rem(x + k, along_x)], b_second.at[k - 1], rows=row_at(k, 0, 0))
        for k in (2, 1, 3)
    ]
    wait(a1)
    a_first_sum[...] = gram[0, x] + a_first[0] + a_first[1] + a_first[2]
    a2 = [send(a_first_sum.at[:, other_z], a_second, rows=row_at(0, 0, 1))]
    wait(s2)
    s_second_sum[...] = s_first_sum[...] + jnp.sum(s_second[...], axis=0)
    s3 = [send(s_second_sum, s_third.at[k], cols=there) for k, there in enumerate(others)]
    wait(a2)
    a_second_sum[...] = a_first_sum[:, z] + a_second[...]
    a3 = [
        send(a_second_sum.at[lax.rem(y + k, 8)], a_third.at[k - 1], rows=y_rows[k - 1])
        for k in (4, 3, 5, 2, 6, 1, 7)
    ]
    wait(b2)
    b_second_sum[...] = b_first_sum[x] + b_second[0] + b_second[1] + b_second[2]
    b3 = [
        send(b_second_sum.at[lax.rem(y + k, 8)], b_third.at[k - 1], rows=y_rows[k - 1])
        for k in (4, 3, 5, 2, 6, 1, 7)
    ]
    wait(s3)
    mine = s_second_sum[...]
    mean_diag = (mine + jnp.sum(s_third[...], axis=0))[4:5, :] / D + epsilon
    scaled = mine * jnp.sqrt(jnp.float32(samples)) / jnp.sqrt(mean_diag * mine[5:6, :])
    rhs_out[...] = scaled[: BW // LANES, :]
    wait(a3)
    left = a_second_sum[y] + jnp.sum(a_third[...], axis=0)
    wait(b3)
    right = b_second_sum[y] + jnp.sum(b_third[...], axis=0)
    for half, block in enumerate((left, right)):
        for j in range(BW // 2 // LANES):
            at = half * (BW // 2) + j * LANES
            gram_out[:, at:at + LANES] = block[:, j * LANES:(j + 1) * LANES] / mean_diag


def finish(gram, small, columns, samples):
    _, nx, ny, nz, height, half = gram.shape
    count = 2 * (nx - 1) + 2 + 2 * (ny - 1) + (nx * nz - 1) + (ny - 1) + (columns - 1)

    def space(*shape):
        return VMEM(shape, jnp.float32)

    tile = small.shape
    return pl.pallas_call(
        functools.partial(finish_kernel, columns, samples),
        out_shape=[
            jax.ShapeDtypeStruct((height, 2 * half), jnp.float32),
            jax.ShapeDtypeStruct((BW // LANES, LANES), jnp.float32),
        ],
        in_specs=[pl.BlockSpec(memory_space=VMEM)] * 2,
        out_specs=[pl.BlockSpec(memory_space=VMEM)] * 2,
        scratch_shapes=[
            space(nx - 1, ny, nz, height, half), space(ny, nz, height, half),
            space(ny, height, half), space(ny, height, half), space(ny - 1, height, half),
            space(nx, ny, height, half), space(nx, ny, height, half),
            space(nx - 1, ny, height, half), space(ny, height, half), space(ny - 1, height, half),
            space(nx * nz - 1, *tile), space(*tile), space(ny - 1, *tile), space(*tile), space(columns - 1, *tile),
            pltpu.SemaphoreType.DMA((count,)),
            pltpu.SemaphoreType.DMA((count,)),
        ],
        compiler_params=pltpu.CompilerParams(collective_id=1, has_side_effects=True),
    )(gram, small)


def local(design, signs, response, picks):
    mixed, answer = trade(*local_mix(design, signs, response))
    gram, small = local_gram(mixed, answer, picks)
    gram_rows, rhs = finish(gram, small, lax.axis_size("cols"), picks.shape[0])
    return (gram_rows[:, None, :], rhs.reshape(BW))


def solution(mesh):
    in_specs = (P("rows", "cols"), P("rows"), P("rows"), P())
    out_specs = (P("rows", "cols", None), P("cols"))
    return jax.shard_map(local, mesh=mesh, in_specs=in_specs, out_specs=out_specs, check_vma=False)
```

time: 150 us -> 110 us (0.73)
  local copies, waits for them, and re-layouts: 16.9 us -> 2.58 us
  matrix products: 12.9 us -> 0 us
  Pallas kernels: 115 us -> 107 us
  other arithmetic: 3.21 us -> 0 us
    dot_general x10 -> x0, matrix products: 12.9 us -> none  [the longest x5 8.1 us: dot(): return jnp.dot(left, right, preferred_element_type=jnp.float32)]
    pallas_call x1 -> x3, Pallas kernels: 50.5 us -> 42 us  [the longest x1 31.4 us: finish(): pl.pallas_call(functools.partial(finish_kernel, columns, samples), out_sh...]
    unnamed x9 -> x2, local copies, waits for them, and re-layouts: 7.89 us -> 2.58 us
    reshape x4 -> x0, local copies, waits for them, and re-layouts: 3.14 us -> none  [the longest x1 1.75 us: local(): mix(groups, mixed.reshape(groups, share * width)).reshape(height, width)]
    convert_element_type x2 -> x0, local copies, waits for them, and re-layouts: 2.86 us -> none  [halves(): return (top.astype(jnp.bfloat16), rest.astype(jnp.bfloat16))]
    concatenate x3 -> x0, local copies, waits for them, and re-layouts: 1.51 us -> none  [local(): jnp.concatenate([rhs_part.reshape(BW // LANES, LANES), jnp.full((1, LANES...]
where the time goes in v3:
time: 110 us
  Pallas kernels  107 us (97%)
  local copies, waits for them, and re-layouts  2.58 us (2%)
    pallas_call x1, Pallas kernels, trade(): pl.pallas_call(functools.partial(trade_kernel, groups), out_shape=[jax.Sh...  64.8 us
    pallas_call x1, Pallas kernels, finish(): pl.pallas_call(functools.partial(finish_kernel, columns, samples), out_sh...  31.4 us
    pallas_call x1, Pallas kernels, local_gram(): pl.pallas_call(gram_kernel, out_shape=[jax.ShapeDtypeStruct((2, groups //...  6.48 us
    pallas_call x1, Pallas kernels, local_mix(): pl.pallas_call(mix_kernel, out_shape=[jax.ShapeDtypeStruct((64, height //...  4.11 us
    unnamed x2, local copies, waits for them, and re-layouts  2.58 us

profile of v3, /device:TPU:1, one launch (start us, length us, event | category | flops | bytes accessed | tf_op | source)
XLA Modules:
  0.0 110.0 jit_solution(6143800846357402247)
XLA Ops:
  0.6 4.1 %shard_map.59 = (f32[64,16,512]{2,1,0:T(8,128)}, f32[8,1,128]{2,1,0:T(1,128)}) custom-call(f32[1024,512]{1,0:T(8,128)} %design.1, s32[8,128]{1,0:T(8,128)} %bitcast.7, f32[8,128]{1,0:T(8,128)} %bitcast.8), custom_call_target="tpu_custom_call" | custom-call | tf_op jit(solution)/shard_map/pallas_call | solution.py:149
  4.7 64.8 %shard_map.60 = (f32[64,16,512]{2,1,0:T(8,128)}, f32[64,1,128]{2,1,0:T(1,128)}) custom-call(f32[64,16,512]{2,1,0:T(8,128)} %get-tuple-element.10.mixed, f32[8,1,128]{2,1,0:T(1,128)} %get-tuple-element.11.answer), custom_call_target="tpu_custom_call" | custom-call | tf_op jit(solution)/shard_map/pallas_call | solution.py:108
  69.5 6.5 %shard_map.61 = (f32[2,4,8,2,8,256]{5,4,3,2,1,0:T(8,128)}, f32[8,128]{1,0:T(8,128)}) custom-call(f32[64,16,512]{2,1,0:T(8,128)} %get-tuple-element.12.mixed, f32[64,1,128]{2,1,0:T(1,128)} %get-tuple-element.13.answer, s32[1,8192]{1,0:T(1,128)} %bitcast.5), custom_call_target="tpu_custom_call" | custom-call | tf_op jit(solution)/shard_map/pallas_call | solution.py:226
  76.0 31.4 %shard_map.62 = (f32[8,512]{1,0:T(8,128)}, f32[4,128]{1,0:T(4,128)}) custom-call(f32[2,4,8,2,8,256]{5,4,3,2,1,0:T(8,128)} %get-tuple-element.14.gram, f32[8,128]{1,0:T(8,128)} %get-tuple-element.15.small), custom_call_target="tpu_custom_call" | custom-call | tf_op jit(solution)/shard_map/pallas_call | solution.py:345
  107.4 1.3 %copy.6 = f32[8,1,512]{2,1,0:T(1,128)} copy(f32[8,1,512]{2,0,1:T(8,128)} %bitcast.6) | data formatting | bytes 32768
  108.8 1.2 %copy.8 = f32[512]{0:T(512)} copy(f32[512]{0:T(512)} %bitcast.9) | data formatting | bytes 4096

commit v4 on v3

--- a/solution.py
+++ b/solution.py
@@ -81,30 +81,105 @@
     return barrier
 
 
-def trade_kernel(groups, mixed, answer, mixed_out, answer_out, sends, receives, answer_sends, answer_receives, own):
+def trade_kernel(
+    groups, mixed, answer, mixed_out, answer_out, relayed,
+    sends, receives, answer_sends, answer_receives, relay_sends, relay_receives, own, hop,
+):
     me = lax.axis_index("rows")
+    along_x = groups // 16
+    half = mixed.shape[3] // 2
+    x = me // 16
+    y = lax.rem(me // 2, 8)
+    z = lax.rem(me, 2)
     pl.semaphore_wait(greet_rows(groups), groups - 1)
 
-    def start(there):
-        to_row(mixed.at[there], mixed_out, sends, receives, me, there).start()
-        to_row(answer.at[there // 8], answer_out, answer_sends, answer_receives, me, there).start()
-
-    def finish(there):
-        to_row(mixed.at[there], mixed_out, sends, receives, there, there).wait()
-        to_row(answer.at[there // 8], answer_out, answer_sends, answer_receives, there, there).wait()
-
-    each_peer(groups, start)
-    keep = pltpu.make_async_copy(mixed.at[me], mixed_out.at[me], own.at[0])
+    def at_row(px, ky, pz):
+        return px * 16 + lax.rem(y + ky, 8) * 2 + pz
+
+    def chunk(there):
+        return mixed.at[there // 16, lax.rem(there // 2, 8), lax.rem(there, 2)]
+
+    def send(slot, there):
+        return to_row(chunk(there), mixed_out, sends, receives, slot, there)
+
+    def send_late_half(slot, there):
+        return pltpu.make_async_remote_copy(
+            src_ref=chunk(there).at[pl.ds(half, half)],
+            dst_ref=mixed_out.at[slot, pl.ds(half, half)],
+            send_sem=sends.at[there],
+            recv_sem=receives.at[slot],
+            device_id={"rows": there},
+            device_id_type=MESH,
+        )
+
+    def send_answer(slot, there):
+        return to_row(answer.at[there // 8], answer_out, answer_sends, answer_receives, slot, there)
+
+    def every(send_one):
+        def plane(j, carry):
+            px = lax.rem(x + j // 2, along_x)
+            pz = lax.rem(z + lax.rem(j, 2), 2)
+            for ky in (4, 3, 5, 2, 6, 1, 7):
+                there = at_row(px, ky, pz)
+                send_one(send_late_half if ky == 4 else send, there)
+                send_one(send_answer, there)
+            return carry
+
+        def level(j, carry):
+            there = at_row(lax.rem(x + j // 2, along_x), 0, lax.rem(z + lax.rem(j, 2), 2))
+            send_one(send, there)
+            send_one(send_answer, there)
+            return carry
+
+        lax.fori_loop(0, 2 * along_x, plane, 0)
+        lax.fori_loop(1, 2 * along_x, level, 0)
+
+    to_relay = pltpu.make_async_remote_copy(
+        src_ref=mixed.at[:, lax.rem(y + 4, 8), :, pl.ds(0, half)],
+        dst_ref=relayed,
+        send_sem=hop.at[0],
+        recv_sem=hop.at[1],
+        device_id={"rows": at_row(x, 6, z)},
+        device_id_type=MESH,
+    )
+    to_relay.start()
+    every(lambda copy, there: copy(me, there).start())
+    keep = pltpu.make_async_copy(chunk(me), mixed_out.at[me], own.at[0])
     keep_answer = pltpu.make_async_copy(answer.at[me // 8], answer_out.at[me], own.at[1])
     keep.start()
     keep_answer.start()
     keep.wait()
     keep_answer.wait()
-    each_peer(groups, finish)
+    to_relay.wait()
+
+    def forward(j, slot, receive):
+        px = j // 2
+        pz = lax.rem(j, 2)
+        return pltpu.make_async_remote_copy(
+            src_ref=relayed.at[px, pz],
+            dst_ref=mixed_out.at[slot, pl.ds(0, half)],
+            send_sem=relay_sends.at[j],
+            recv_sem=relay_receives.at[receive],
+            device_id={"rows": at_row(px, 6, pz)},
+            device_id_type=MESH,
+        )
+
+    def pass_on(j, carry):
+        forward(j, at_row(x, 2, z), x * 2 + z).start()
+        return carry
+
+    def take(j, carry):
+        forward(j, at_row(j // 2, 4, lax.rem(j, 2)), j).wait()
+        return carry
+
+    lax.fori_loop(0, 2 * along_x, pass_on, 0)
+    every(lambda copy, there: copy(there, there).wait())
+    lax.fori_loop(0, 2 * along_x, take, 0)
 
 
 def trade(mixed, answer):
-    groups = mixed.shape[0]
+    groups, share, width = mixed.shape
+    planes = 2 * (groups // 16)
     return pl.pallas_call(
         functools.partial(trade_kernel, groups),
         out_shape=[
@@ -113,9 +188,12 @@
         ],
         in_specs=[pl.BlockSpec(memory_space=VMEM)] * 2,
         out_specs=[pl.BlockSpec(memory_space=VMEM)] * 2,
-        scratch_shapes=[pltpu.SemaphoreType.DMA((groups,))] * 4 + [pltpu.SemaphoreType.DMA((2,))],
+        scratch_shapes=[VMEM((groups // 16, 2, share // 2, width), jnp.float32)]
+        + [pltpu.SemaphoreType.DMA((groups,))] * 4
+        + [pltpu.SemaphoreType.DMA((planes,))] * 2
+        + [pltpu.SemaphoreType.DMA((2,))] * 2,
         compiler_params=pltpu.CompilerParams(collective_id=0, has_side_effects=True),
-    )(mixed, answer)
+    )(mixed.reshape(groups // 16, 8, 2, share, width), answer)
 
 
 def mix_kernel(design, signs, response, mixed, answer):

time: 110 us -> 115 us (1.045)
  Pallas kernels: 107 us -> 111 us
    pallas_call x1, Pallas kernels: 64.8 us -> 68.5 us  [trade(): pl.pallas_call(functools.partial(trade_kernel, groups), out_shape=[jax.Sh...]
where the time goes in v4:
time: 115 us; the launch traced here: 114 us
  Pallas kernels  111 us (97%)
  local copies, waits for them, and re-layouts  2.58 us (2%)
    pallas_call x1, Pallas kernels, trade(): pl.pallas_call(functools.partial(trade_kernel, groups), out_shape=[jax.Sh...  68.5 us
    pallas_call x1, Pallas kernels, finish(): pl.pallas_call(functools.partial(finish_kernel, columns, samples), out_sh...  31.9 us
    pallas_call x1, Pallas kernels, local_gram(): pl.pallas_call(gram_kernel, out_shape=[jax.ShapeDtypeStruct((2, groups //...  6.48 us
    pallas_call x1, Pallas kernels, local_mix(): pl.pallas_call(mix_kernel, out_shape=[jax.ShapeDtypeStruct((64, height //...  4.11 us
    unnamed x2, local copies, waits for them, and re-layouts  2.58 us

profile of v4, /device:TPU:1, one launch (start us, length us, event | category | flops | bytes accessed | tf_op | source)
XLA Modules:
  0.0 114.2 jit_solution(6965117662197249030)
XLA Ops:
  0.6 4.1 %shard_map.59 = (f32[64,16,512]{2,1,0:T(8,128)}, f32[8,1,128]{2,1,0:T(1,128)}) custom-call(f32[1024,512]{1,0:T(8,128)} %design.1, s32[8,128]{1,0:T(8,128)} %bitcast.9, f32[8,128]{1,0:T(8,128)} %bitcast.10), custom_call_target="tpu_custom_call" | custom-call | tf_op jit(solution)/shard_map/pallas_call | solution.py:227
  4.7 68.5 %shard_map.60 = (f32[64,16,512]{2,1,0:T(8,128)}, f32[64,1,128]{2,1,0:T(1,128)}) custom-call(f32[4,8,2,16,512]{4,3,2,1,0:T(8,128)} %bitcast.6, f32[8,1,128]{2,1,0:T(1,128)} %get-tuple-element.11.answer), custom_call_target="tpu_custom_call" | custom-call | tf_op jit(solution)/shard_map/pallas_call | solution.py:183
  73.2 6.5 %shard_map.61 = (f32[2,4,8,2,8,256]{5,4,3,2,1,0:T(8,128)}, f32[8,128]{1,0:T(8,128)}) custom-call(f32[64,16,512]{2,1,0:T(8,128)} %get-tuple-element.12.mixed, f32[64,1,128]{2,1,0:T(1,128)} %get-tuple-element.13.answer, s32[1,8192]{1,0:T(1,128)} %bitcast.7), custom_call_target="tpu_custom_call" | custom-call | tf_op jit(solution)/shard_map/pallas_call | solution.py:304
  79.7 31.9 %shard_map.62 = (f32[8,512]{1,0:T(8,128)}, f32[4,128]{1,0:T(4,128)}) custom-call(f32[2,4,8,2,8,256]{5,4,3,2,1,0:T(8,128)} %get-tuple-element.14.gram, f32[8,128]{1,0:T(8,128)} %get-tuple-element.15.small), custom_call_target="tpu_custom_call" | custom-call | tf_op jit(solution)/shard_map/pallas_call | solution.py:423
  111.6 1.3 %copy.6 = f32[8,1,512]{2,1,0:T(1,128)} copy(f32[8,1,512]{2,0,1:T(8,128)} %bitcast.8) | data formatting | bytes 32768
  112.9 1.2 %copy.8 = f32[512]{0:T(512)} copy(f32[512]{0:T(512)} %bitcast.11) | data formatting | bytes 4096

commit v5 on v3

--- a/solution.py
+++ b/solution.py
@@ -81,8 +81,12 @@
     return barrier
 
 
-def trade_kernel(groups, mixed, answer, mixed_out, answer_out, sends, receives, answer_sends, answer_receives, own):
+def trade_kernel(
+    groups, mixed, answer, picks, mixed_out, answer_out, picked,
+    sends, receives, answer_sends, answer_receives, own,
+):
     me = lax.axis_index("rows")
+    share = mixed.shape[1]
     pl.semaphore_wait(greet_rows(groups), groups - 1)
 
     def start(there):
@@ -98,24 +102,35 @@
     keep_answer = pltpu.make_async_copy(answer.at[me // 8], answer_out.at[me], own.at[1])
     keep.start()
     keep_answer.start()
+    wanted = picks[...]
+    group_of = jnp.right_shift(wanted, 10)
+    inside = jnp.bitwise_and(wanted, groups * share - 1) - me * share
+    samples = wanted.shape[1]
+    of_group = (lax.broadcasted_iota(jnp.int32, (groups, samples), 0) == group_of).astype(jnp.float32)
+    of_local = (lax.broadcasted_iota(jnp.int32, (share, samples), 0) == inside).astype(jnp.float32)
+    picked[...] = lax.dot_general(
+        of_group.astype(jnp.bfloat16), of_local.astype(jnp.bfloat16), (((1,), (1,)), ((), ())),
+        preferred_element_type=jnp.float32,
+    )
     keep.wait()
     keep_answer.wait()
     each_peer(groups, finish)
 
 
-def trade(mixed, answer):
+def trade(mixed, answer, picks):
     groups = mixed.shape[0]
     return pl.pallas_call(
         functools.partial(trade_kernel, groups),
         out_shape=[
             jax.ShapeDtypeStruct(mixed.shape, jnp.float32),
             jax.ShapeDtypeStruct((groups, 1, LANES), jnp.float32),
-        ],
-        in_specs=[pl.BlockSpec(memory_space=VMEM)] * 2,
-        out_specs=[pl.BlockSpec(memory_space=VMEM)] * 2,
+            jax.ShapeDtypeStruct((groups, mixed.shape[1]), jnp.float32),
+        ],
+        in_specs=[pl.BlockSpec(memory_space=VMEM)] * 3,
+        out_specs=[pl.BlockSpec(memory_space=VMEM)] * 3,
         scratch_shapes=[pltpu.SemaphoreType.DMA((groups,))] * 4 + [pltpu.SemaphoreType.DMA((2,))],
         compiler_params=pltpu.CompilerParams(collective_id=0, has_side_effects=True),
-    )(mixed, answer)
+    )(mixed, answer, picks.reshape(1, -1))
 
 
 def mix_kernel(design, signs, response, mixed, answer):
@@ -157,7 +172,7 @@
     )(design, signs.reshape(blocks, LANES), response.reshape(blocks, LANES))
 
 
-def gram_kernel(mixed, answer, picks, gram, small, held):
+def gram_kernel(mixed, answer, picked, gram, small, held):
     groups, share, width = mixed.shape
     height = groups * share
     position = lax.axis_index("rows")
@@ -182,19 +197,9 @@
         sylvester(groups, jnp.float32), answer[:, 0, :],
         precision=lax.Precision.HIGHEST, preferred_element_type=jnp.float32,
     )
-    wanted = picks[...]
-    group_of = jnp.right_shift(wanted, 10)
-    inside = jnp.bitwise_and(wanted, height - 1) - position * share
-    samples = wanted.shape[1]
-    of_group = (lax.broadcasted_iota(jnp.int32, (groups, samples), 0) == group_of).astype(jnp.float32)
-    of_local = (lax.broadcasted_iota(jnp.int32, (LANES, samples), 0) == inside).astype(jnp.float32)
-    picked = lax.dot_general(
-        of_group.astype(jnp.bfloat16), of_local[:share].astype(jnp.bfloat16), (((1,), (1,)), ((), ())),
-        preferred_element_type=jnp.float32,
-    )
     lane = lax.broadcasted_iota(jnp.int32, (groups, share, share), 2)
     local_row = lax.broadcasted_iota(jnp.int32, (groups, share, share), 1)
-    picked_rows = jnp.sum(jnp.where(lane == local_row, picked[:, None, :], 0.0), axis=2, keepdims=True)
+    picked_rows = jnp.sum(jnp.where(lane == local_row, picked[...][:, None, :], 0.0), axis=2, keepdims=True)
     lane = lax.broadcasted_iota(jnp.int32, (groups, share, LANES), 2)
     local_row = lax.broadcasted_iota(jnp.int32, (groups, share, LANES), 1) + lax.rem(position, 8) * share
     answer_rows = jnp.sum(jnp.where(lane == local_row, mixed_answer[:, None, :], 0.0), axis=2, keepdims=True)
@@ -221,7 +226,7 @@
     small[6:8, :] = jnp.zeros((2, LANES), jnp.float32)
 
 
-def local_gram(mixed, answer, picks):
+def local_gram(mixed, answer, picked):
     groups, share, width = mixed.shape
     return pl.pallas_call(
         gram_kernel,
@@ -233,7 +238,7 @@
         out_specs=[pl.BlockSpec(memory_space=VMEM)] * 2,
         scratch_shapes=[VMEM(mixed.shape, jnp.float32)],
         compiler_params=pltpu.CompilerParams(vmem_limit_bytes=60 * 2**20),
-    )(mixed, answer, picks.reshape(1, -1))
+    )(mixed, answer, picked)
 
 
 def finish_kernel(
@@ -364,8 +369,8 @@
 
 
 def local(design, signs, response, picks):
-    mixed, answer = trade(*local_mix(design, signs, response))
-    gram, small = local_gram(mixed, answer, picks)
+    mixed, answer, picked = trade(*local_mix(design, signs, response), picks)
+    gram, small = local_gram(mixed, answer, picked)
     gram_rows, rhs = finish(gram, small, lax.axis_size("cols"), picks.shape[0])
     return (gram_rows[:, None, :], rhs.reshape(BW))
 

time: 110 us -> 110 us (level)
  no operation moved by 1% of the time
where the time goes in v5:
time: 110 us; the launch traced here: 109 us
  Pallas kernels  106 us (96%)
  local copies, waits for them, and re-layouts  2.58 us (2%)
    pallas_call x1, Pallas kernels, trade(): pl.pallas_call(functools.partial(trade_kernel, groups), out_shape=[jax.Sh...  64.8 us
    pallas_call x1, Pallas kernels, finish(): pl.pallas_call(functools.partial(finish_kernel, columns, samples), out_sh...  31.4 us
    pallas_call x1, Pallas kernels, local_gram(): pl.pallas_call(gram_kernel, out_shape=[jax.ShapeDtypeStruct((2, groups //...  5.78 us
    pallas_call x1, Pallas kernels, local_mix(): pl.pallas_call(mix_kernel, out_shape=[jax.ShapeDtypeStruct((64, height //...  4.11 us
    unnamed x2, local copies, waits for them, and re-layouts  2.58 us

profile of v5, /device:TPU:1, one launch (start us, length us, event | category | flops | bytes accessed | tf_op | source)
XLA Modules:
  0.0 109.3 jit_solution(17980393879735581564)
XLA Ops:
  0.6 4.1 %shard_map.59 = (f32[64,16,512]{2,1,0:T(8,128)}, f32[8,1,128]{2,1,0:T(1,128)}) custom-call(f32[1024,512]{1,0:T(8,128)} %design.1, s32[8,128]{1,0:T(8,128)} %bitcast.7, f32[8,128]{1,0:T(8,128)} %bitcast.8), custom_call_target="tpu_custom_call" | custom-call | tf_op jit(solution)/shard_map/pallas_call | solution.py:164
  4.7 64.8 %shard_map.60 = (f32[64,16,512]{2,1,0:T(8,128)}, f32[64,1,128]{2,1,0:T(1,128)}, f32[64,16]{1,0:T(8,128)}) custom-call(f32[64,16,512]{2,1,0:T(8,128)} %get-tuple-element.11.mixed, f32[8,1,128]{2,1,0:T(1,128)} %get-tuple-element.12.answer, s32[1,8192]{1,0:T(1,128)} %bitcast.5), custom_call_target="tpu_custom_call" | custom-call | tf_op jit(solution)/shard_map/pallas_call | solution.py:122
  69.5 5.8 %shard_map.61 = (f32[2,4,8,2,8,256]{5,4,3,2,1,0:T(8,128)}, f32[8,128]{1,0:T(8,128)}) custom-call(f32[64,16,512]{2,1,0:T(8,128)} %get-tuple-element.13.mixed, f32[64,1,128]{2,1,0:T(1,128)} %get-tuple-element.14.answer, f32[64,16]{1,0:T(8,128)} %get-tuple-element.15.picked), custom_call_target="tpu_custom_call" | custom-call | tf_op jit(solution)/shard_map/pallas_call | solution.py:231
  75.3 31.4 %shard_map.62 = (f32[8,512]{1,0:T(8,128)}, f32[4,128]{1,0:T(4,128)}) custom-call(f32[2,4,8,2,8,256]{5,4,3,2,1,0:T(8,128)} %get-tuple-element.16.gram, f32[8,128]{1,0:T(8,128)} %get-tuple-element.17.small), custom_call_target="tpu_custom_call" | custom-call | tf_op jit(solution)/shard_map/pallas_call | solution.py:350
  106.7 1.3 %copy.6 = f32[8,1,512]{2,1,0:T(1,128)} copy(f32[8,1,512]{2,0,1:T(8,128)} %bitcast.6) | data formatting | bytes 32768
  108.1 1.2 %copy.8 = f32[512]{0:T(512)} copy(f32[512]{0:T(512)} %bitcast.9) | data formatting | bytes 4096

commit v6 on v5

--- a/solution.py
+++ b/solution.py
@@ -55,7 +55,7 @@
 
 def each_peer(groups, action):
     def step(k, carry):
-        action(peer(groups, k))
+        action(peer(groups, lax.rem(k * 27, groups)))
         return carry
 
     lax.fori_loop(1, groups, step, 0)

time: 110 us -> 110 us (level)
    pallas_call x1, Pallas kernels: 31.4 us -> 30 us  [finish(): pl.pallas_call(functools.partial(finish_kernel, columns, samples), out_sh...]
    pallas_call x1, Pallas kernels: 64.8 us -> 66.1 us  [trade(): pl.pallas_call(functools.partial(trade_kernel, groups), out_shape=[jax.Sh...]
where the time goes in v6:
time: 110 us; the launch traced here: 109 us
  Pallas kernels  106 us (96%)
  local copies, waits for them, and re-layouts  2.58 us (2%)
    pallas_call x1, Pallas kernels, trade(): pl.pallas_call(functools.partial(trade_kernel, groups), out_shape=[jax.Sh...  66.1 us
    pallas_call x1, Pallas kernels, finish(): pl.pallas_call(functools.partial(finish_kernel, columns, samples), out_sh...  30 us
    pallas_call x1, Pallas kernels, local_gram(): pl.pallas_call(gram_kernel, out_shape=[jax.ShapeDtypeStruct((2, groups //...  5.77 us
    pallas_call x1, Pallas kernels, local_mix(): pl.pallas_call(mix_kernel, out_shape=[jax.ShapeDtypeStruct((64, height //...  4.11 us
    unnamed x2, local copies, waits for them, and re-layouts  2.58 us

profile of v6, /device:TPU:1, one launch (start us, length us, event | category | flops | bytes accessed | tf_op | source)
XLA Modules:
  0.0 109.3 jit_solution(17958727681314406665)
XLA Ops:
  0.6 4.1 %shard_map.59 = (f32[64,16,512]{2,1,0:T(8,128)}, f32[8,1,128]{2,1,0:T(1,128)}) custom-call(f32[1024,512]{1,0:T(8,128)} %design.1, s32[8,128]{1,0:T(8,128)} %bitcast.7, f32[8,128]{1,0:T(8,128)} %bitcast.8), custom_call_target="tpu_custom_call" | custom-call | tf_op jit(solution)/shard_map/pallas_call | solution.py:164
  4.7 66.1 %shard_map.60 = (f32[64,16,512]{2,1,0:T(8,128)}, f32[64,1,128]{2,1,0:T(1,128)}, f32[64,16]{1,0:T(8,128)}) custom-call(f32[64,16,512]{2,1,0:T(8,128)} %get-tuple-element.11.mixed, f32[8,1,128]{2,1,0:T(1,128)} %get-tuple-element.12.answer, s32[1,8192]{1,0:T(1,128)} %bitcast.5), custom_call_target="tpu_custom_call" | custom-call | tf_op jit(solution)/shard_map/pallas_call | solution.py:122
  70.9 5.8 %shard_map.61 = (f32[2,4,8,2,8,256]{5,4,3,2,1,0:T(8,128)}, f32[8,128]{1,0:T(8,128)}) custom-call(f32[64,16,512]{2,1,0:T(8,128)} %get-tuple-element.13.mixed, f32[64,1,128]{2,1,0:T(1,128)} %get-tuple-element.14.answer, f32[64,16]{1,0:T(8,128)} %get-tuple-element.15.picked), custom_call_target="tpu_custom_call" | custom-call | tf_op jit(solution)/shard_map/pallas_call | solution.py:231
  76.7 30.0 %shard_map.62 = (f32[8,512]{1,0:T(8,128)}, f32[4,128]{1,0:T(4,128)}) custom-call(f32[2,4,8,2,8,256]{5,4,3,2,1,0:T(8,128)} %get-tuple-element.16.gram, f32[8,128]{1,0:T(8,128)} %get-tuple-element.17.small), custom_call_target="tpu_custom_call" | custom-call | tf_op jit(solution)/shard_map/pallas_call | solution.py:350
  106.7 1.3 %copy.6 = f32[8,1,512]{2,1,0:T(1,128)} copy(f32[8,1,512]{2,0,1:T(8,128)} %bitcast.6) | data formatting | bytes 32768
  108.0 1.2 %copy.8 = f32[512]{0:T(512)} copy(f32[512]{0:T(512)} %bitcast.9) | data formatting | bytes 4096
